TPU v7x, 256 devices: a whole 4x4x8 slice. The times are simulated.
256 devices in a mesh: row: 16 (over x, z_hi, core), col: 16 (over z_lo, y).
Axes of the slice: x: 4, y: 4, z: 8 (z_hi: 2, z_lo: 4; z = z_hi * 4 + z_lo), core: 2. Of those that a mesh axis runs over, the one named last changes fastest.
Arguments:
- ancestor_inverse: bfloat16 [24576, 24576], P('row', 'col'), may hold values from -0.0390625 to 0.0390625
- panels: bfloat16 [24576, 3, 512], P(('row', 'col')), may hold values from -1.1953125 to 1.1953125
- diag_inverse: float32 [3, 512, 512], replicated, may hold values from -6 to 6
- tile_mask: int32 [3, 192], replicated, may hold values 0 or 1
Outputs:
- off_diagonal: float32 [24576, 3, 512], P(('row', 'col'))
- diagonal: float32 [3, 512, 512], replicated
All inputs are finite; a program needn't handle non-finite values.
Results may differ from a plain program's by a relative error of at most 0.0003.
Values may be sent and summed in bfloat16 or wider, within the bound.
No kernel may reach another device: no remote copies, remote signals or barrier semaphores. Data moves between devices by JAX's collectives and lax.ppermute only.
A program may use at most 192 MiB of HBM per device.

v0:
```python
import jax
import jax.numpy as jnp
from jax import lax
from jax.sharding import Mesh
from jax.sharding import PartitionSpec as P

TILE = 128
COL = ("col_0", "col_1")
ROW_COL = ("row", "col_0", "col_1")


def in_order(tiles, dim):
    tiles = jnp.moveaxis(tiles, 0, dim)
    dims = tiles.shape
    return tiles.reshape(*dims[:dim], dims[dim] * dims[dim + 1], *dims[dim + 2 :])


def stacked_from(shard, axes, sequence):
    tiles = shard
    for k in sequence:
        tiles = lax.all_gather(tiles, axes[k])
    done = sequence[::-1]
    back = [done.index(k) for k in range(len(axes))]
    tiles = tiles.transpose(*back, *range(len(axes), tiles.ndim))
    return tiles.reshape(-1, *shard.shape)


def gathered_by_axis(shard, axes, sequence, dim):
    return in_order(stacked_from(shard, axes, sequence), dim)


def filled_up(lines, devices):
    spare = -lines.shape[0] % devices
    if not spare:
        return lines
    return jnp.concatenate([lines, jnp.zeros((spare, *lines.shape[1:]), lines.dtype)])


def from_root(shard, axis, root):
    lines = jnp.where(lax.axis_index(axis) == root, shard, jnp.zeros_like(shard)).reshape(
        -1, *shard.shape[1:][-1:]
    )
    padded = filled_up(lines, lax.axis_size(axis))
    own = lax.psum_scatter(padded, axis, scatter_dimension=0, tiled=True)
    return lax.all_gather(own, axis, axis=0, tiled=True)[: len(lines)].reshape(shard.shape)


def make_term(ancestor_inverse, right_side):
    return jnp.dot(ancestor_inverse, right_side, preferred_element_type=jnp.float32)


def body(ancestor_inverse, panels, diag_inverse, tile_mask):
    row_count = lax.axis_size("row")
    col_count = lax.axis_size(COL)
    col_index = lax.axis_index(COL)
    row_index = lax.axis_index("row")
    kept_rows = panels.shape[0]
    panel_count = panels.shape[1]
    width_cols = panels.shape[2]
    matrix_order = kept_rows * row_count * col_count
    block_rows = matrix_order // col_count
    full_mask = jnp.repeat(tile_mask, TILE, axis=1).T.astype(jnp.bfloat16)
    gathered = gathered_by_axis(panels, COL, (0, 1), 0)
    col_group = col_count // row_count
    root_row = col_index // col_group
    partner = from_root(gathered, "row", root_row)
    col_mask = lax.dynamic_slice_in_dim(full_mask, col_index * block_rows, block_rows, 0)
    masked_col = partner * col_mask[:, :, None]
    flattened = masked_col.reshape(block_rows, panel_count * width_cols)
    summed = lax.psum_scatter(
        make_term(ancestor_inverse, flattened), COL, scatter_dimension=0, tiled=True
    )
    off_diagonal = -summed.reshape(kept_rows, panel_count, width_cols)
    span_start = (row_index * col_count + col_index) * kept_rows
    own_mask = lax.dynamic_slice_in_dim(full_mask, span_start, kept_rows, 0)
    masked_own = (panels * own_mask[:, :, None]).astype(jnp.float32)
    schur_part = jnp.einsum(
        "mpa,mpb->pab", masked_own, off_diagonal, precision=lax.Precision.HIGHEST
    )
    schur_total = lax.psum(schur_part, ROW_COL)
    diagonal = diag_inverse - schur_total
    return (off_diagonal, diagonal)


def solution(mesh):
    finer = Mesh(mesh.devices.reshape(mesh.shape["row"], 4, 4), ("row", "col_0", "col_1"))
    placed = (P("row", COL), P(ROW_COL, None, None), P(), P())
    return jax.shard_map(
        body, mesh=finer, in_specs=placed, out_specs=(P(ROW_COL, None, None), P()), check_vma=False
    )
```

profile of v0, /device:TPU:2, one launch (start us, length us, event | category | flops | bytes accessed | tf_op | source)
XLA Modules:
  0.0 742.1 jit_solution(1819610652847261270)
XLA Ops:
  7.2 0.0 all-gather.8.cloned.1.call-start
  7.2 0.7 all-gather.8.cloned.1.call-update
  7.9 0.0 all-gather.10.cloned.1.call-start
  7.9 40.4 %all-gather.8.cloned.1.call-done = bf16[384,3,512]{2,0,1:T(8,128)(2,1)} async-done(((bf16[96,3,512]{2,0,1:T(8,128)(2,1)}), bf16[384,3,512]{2,0,1:T(8,128)(2,1)}) %all-gather.8.cloned.1.call-update) | async-done | bytes 1179664 | tf_op jit(solution)/shard_map/all_gather | solution.py:21
  48.4 0.0 all-gather.10.cloned.1.call-update
  48.4 0.0 reduce-scatter.5.cloned.1.call-start
  48.4 56.1 %all-gather.10.cloned.1.call-done = bf16[16,96,3,512]{3,1,0,2:T(8,128)(2,1)} async-done(((bf16[4,96,3,512]{3,1,0,2:T(8,128)(2,1)}), bf16[16,96,3,512]{3,1,0,2:T(8,128)(2,1)}) %all-gather.10.cloned.1.call-update) | async-done | bytes 4718608 | tf_op jit(solution)/shard_map/all_gather | solution.py:21
  104.5 0.3 broadcast_select_fusion
  104.8 6.7 copy.22
  111.6 12.3 %select_n.27 = bf16[4608,512]{1,0:T(8,128)(2,1)} reshape(bf16[4,4,96,3,512]{4,3,2,1,0:T(4,128)(2,1)} %copy.22) | data formatting | bytes 9437184 | tf_op jit(solution)/shard_map/jit(_where)/select_n | solution.py:40
  123.9 0.0 copy-start.1
  123.9 0.0 reduce-scatter.5.cloned.1.call-update
  123.9 0.0 all-gather.6.cloned.1.call-start
  124.0 109.4 %reduce-scatter.5.cloned.1.call-done = bf16[288,512]{1,0:T(8,128)(2,1)} async-done(((bf16[4608,512]{1,0:T(8,128)(2,1)}), bf16[288,512]{1,0:T(8,128)(2,1)}) %reduce-scatter.5.cloned.1.call-update) | async-done | bytes 294928 | tf_op jit(solution)/shard_map/reduce_scatter | solution.py:44
  233.4 0.0 all-gather.6.cloned.1.call-update
  233.4 0.0 reduce-scatter.7.cloned.1.call-start
  233.4 0.0 copy-done.1
  233.5 0.1 broadcast_bitcast_fusion
  233.6 0.1 copy.32
  233.8 79.2 %all-gather.6.cloned.1.call-done = bf16[4608,512]{1,0:T(8,128)(2,1)} async-done(((bf16[288,512]{1,0:T(8,128)(2,1)}), bf16[4608,512]{1,0:T(8,128)(2,1)}) %all-gather.6.cloned.1.call-update) | async-done | bytes 4718608 | tf_op jit(solution)/shard_map/all_gather | solution.py:45
  313.0 8.3 %reshape.21 = bf16[1536,1536]{1,0:T(8,128)(2,1)} reshape(bf16[4608,512]{1,0:T(8,128)(2,1)} %all-gather.6.cloned.1.call-done) | data formatting | bytes 9437184 | tf_op jit(solution)/shard_map/reshape | solution.py:45
  321.3 6.6 copy.23
  327.9 2.6 bitcast_multiply_fusion
  330.6 11.9 %convolution_bitcast_fusion = f32[1536,1536]{0,1:T(8,128)} fusion(bf16[1536,1536]{0,1:T(8,128)(2,1)S(1)} %bitcast_multiply_fusion, bf16[1536,1536]{1,0:T(8,128)(2,1)} %param.4), kind=kOutput, calls=%fused_computation | convolution fusion | flops 7247757312 | bytes 18874368 | tf_op jit(solution)/shard_map/dot_general | solution.py:49
  342.5 9.6 %copy.28 = f32[1536,1536]{1,0:T(8,128)} copy(f32[1536,1536]{0,1:T(8,128)} %convolution_bitcast_fusion) | data formatting | bytes 18874368
  352.2 0.0 copy-start
  352.2 0.0 reduce-scatter.7.cloned.1.call-update
  352.2 0.2 all-reduce.2.cloned.1.call-start
  352.5 0.1 dynamic-slice_bitcast_fusion.1
  352.5 108.9 %reduce-scatter.7.cloned.1.call-done = f32[96,1536]{1,0:T(8,128)} async-done(((f32[1536,1536]{1,0:T(8,128)}), f32[96,1536]{1,0:T(8,128)}) %reduce-scatter.7.cloned.1.call-update) | async-done | bytes 589840
  461.4 1.3 copy.29
  462.8 0.1 neg.6
  462.8 0.0 copy-done
  462.8 3.3 fusion
  466.1 0.0 all-reduce.2.cloned.1.call-update
  466.1 1.1 copy.25
  467.2 262.8 %all-reduce.2.cloned.1.call-done = f32[3,512,512]{2,1,0:T(8,128)} async-done(((f32[3,512,512]{2,1,0:T(8,128)}), f32[3,512,512]{2,1,0:T(8,128)}) %all-reduce.2.cloned.1.call-update) | async-done | bytes 3145744 | tf_op jit(solution)/shard_map/psum | solution.py:80
  730.0 5.3 sub.5
  (2 shorter events, 0.0 us)
Async XLA Ops:
  7.2 41.2 %all-gather.8.cloned.1.call-start = ((), (), s32[]{:S(2)}) async-start(), calls=%async_computation.5 | async-start | bytes 1474560 | tf_op jit(solution)/shard_map/all_gather | solution.py:21
  7.9 96.6 %all-gather.10.cloned.1.call-start = ((), (), s32[]{:S(2)}) async-start(), calls=%async_computation.6 | async-start | bytes 5898240 | tf_op jit(solution)/shard_map/all_gather | solution.py:21
  48.4 185.0 %reduce-scatter.5.cloned.1.call-start = ((), (), s32[]{:S(2)}) async-start(), calls=%async_computation.2 | async-start | bytes 5013504 | tf_op jit(solution)/shard_map/reduce_scatter | solution.py:44
  123.9 109.6 %copy-start.1 = (s32[3,192]{1,0:T(4,128)S(1)}, s32[3,192]{1,0:T(4,128)}, u32[]{:S(2)}) copy-start(s32[3,192]{1,0:T(4,128)} %param.7) | copy-start | bytes 6916
  123.9 189.1 %all-gather.6.cloned.1.call-start = ((), (), s32[]{:S(2)}) async-start(), calls=%async_computation.3 | async-start | bytes 5013504 | tf_op jit(solution)/shard_map/all_gather | solution.py:45
  233.4 228.0 %reduce-scatter.7.cloned.1.call-start = ((), (), s32[]{:S(2)}) async-start(), calls=%async_computation.7 | async-start | bytes 10027008
  352.2 110.6 %copy-start = (bf16[96,3,512]{2,0,1:T(8,128)(2,1)S(1)}, bf16[96,3,512]{2,0,1:T(8,128)(2,1)}, u32[]{:S(2)}) copy-start(bf16[96,3,512]{2,0,1:T(8,128)(2,1)} %param.5) | copy-start | bytes 884740
  352.2 377.8 %all-reduce.2.cloned.1.call-start = ((), (), s32[]{:S(2)}) async-start(), calls=%async_computation.4 | async-start | bytes 6291456 | tf_op jit(solution)/shard_map/psum | solution.py:80
Sparse Core Ops, SparseCore 0:
  9.8 38.5 all-gather.7
  50.2 54.3 all-gather.9
  124.0 109.2 reduce-scatter.4
  236.3 76.6 all-gather.5
  352.3 109.0 reduce-scatter.6
  468.2 261.7 all-reduce.1
where the time goes:
time: 743 us; the launch traced here: 742 us
  waiting for transfers between devices  658 us (89%)
  local copies, waits for them, and re-layouts  46.4 us (6%)
  matrix products  15.2 us (2%)
  between operations  14.2 us (2%)
  other arithmetic  8.27 us (1%)
    psum x1, waiting for transfers between devices, body(): schur_total = lax.psum(schur_part, ROW_COL)  263 us
    unnamed x7, waiting for transfers between devices  110 us
    reduce_scatter x1, waiting for transfers between devices, from_root(): own = lax.psum_scatter(padded, axis, scatter_dimension=0, tiled=True)  109 us
    all_gather x2, waiting for transfers between devices, stacked_from(): tiles = lax.all_gather(tiles, axes[k])  96.5 us
    all_gather x1, waiting for transfers between devices, from_root(): lax.all_gather(own, axis, axis=0, tiled=True)[:len(lines)]  79.2 us
    select_n x2, local copies, waits for them, and re-layouts, from_root(): jnp.where(lax.axis_index(axis) == root, shard, jnp.zeros_like(shard))  19.1 us
    reshape x2, local copies, waits for them, and re-layouts, from_root(): lax.all_gather(own, axis, axis=0, tiled=True)[:len(lines)]  14.9 us
  transfers between devices with their start and end apart: 6, of which 6 were waited for; matrix products, arithmetic and copies ran while one was open for 0% of the time, Pallas kernels for 0%

commit v1 on v0

--- a/solution.py
+++ b/solution.py
@@ -77,7 +77,7 @@
     schur_part = jnp.einsum(
         "mpa,mpb->pab", masked_own, off_diagonal, precision=lax.Precision.HIGHEST
     )
-    schur_total = lax.psum(schur_part, ROW_COL)
+    schur_total = lax.psum(lax.psum(schur_part, ("col_0", "col_1")), "row")
     diagonal = diag_inverse - schur_total
     return (off_diagonal, diagonal)
 

time: 743 us -> 865 us (1.16)
  waiting for transfers between devices: 658 us -> 774 us
    psum x1 -> x2, waiting for transfers between devices: 263 us -> 379 us  [body(): schur_total = lax.psum(lax.psum(schur_part, ('col_0', 'col_1')), 'row')]
    unnamed x7 -> x8, waiting for transfers between devices: 110 us -> 110 us
  transfers between devices with their start and end apart: 6 -> 7, of which waited for: 6 -> 7; matrix products, arithmetic and copies ran while one was open for 0% -> 0% of each run, Pallas kernels for 0% -> 0%
where the time goes in v1:
time: 865 us; the launch traced here: 859 us
  waiting for transfers between devices  774 us (89%)
  local copies, waits for them, and re-layouts  46.4 us (5%)
  matrix products  15.2 us (2%)
  between operations  14.2 us (2%)
    psum x2, waiting for transfers between devices, body(): schur_total = lax.psum(lax.psum(schur_part, ('col_0', 'col_1')), 'row')  379 us
    unnamed x8, waiting for transfers between devices  110 us
    reduce_scatter x1, waiting for transfers between devices, from_root(): own = lax.psum_scatter(padded, axis, scatter_dimension=0, tiled=True)  109 us
    all_gather x2, waiting for transfers between devices, stacked_from(): tiles = lax.all_gather(tiles, axes[k])  96.5 us
    all_gather x1, waiting for transfers between devices, from_root(): lax.all_gather(own, axis, axis=0, tiled=True)[:len(lines)]  79.2 us
    select_n x2, local copies, waits for them, and re-layouts, from_root(): jnp.where(lax.axis_index(axis) == root, shard, jnp.zeros_like(shard))  19.1 us
  transfers between devices with their start and end apart: 7, of which 7 were waited for; matrix products, arithmetic and copies ran while one was open for 0% of the time, Pallas kernels for 0%

profile of v1, /device:TPU:2, one launch (start us, length us, event | category | flops | bytes accessed | tf_op | source)
XLA Modules:
  0.0 858.6 jit_solution(8746964514811693192)
XLA Ops:
  7.2 0.0 all-gather.8.cloned.1.call-start
  7.2 0.7 all-gather.8.cloned.1.call-update
  7.9 0.0 all-gather.10.cloned.1.call-start
  7.9 40.4 %all-gather.8.cloned.1.call-done = bf16[384,3,512]{2,0,1:T(8,128)(2,1)} async-done(((bf16[96,3,512]{2,0,1:T(8,128)(2,1)}), bf16[384,3,512]{2,0,1:T(8,128)(2,1)}) %all-gather.8.cloned.1.call-update) | async-done | bytes 1179664 | tf_op jit(solution)/shard_map/all_gather | solution.py:21
  48.4 0.0 all-gather.10.cloned.1.call-update
  48.4 0.0 reduce-scatter.5.cloned.1.call-start
  48.4 56.1 %all-gather.10.cloned.1.call-done = bf16[16,96,3,512]{3,1,0,2:T(8,128)(2,1)} async-done(((bf16[4,96,3,512]{3,1,0,2:T(8,128)(2,1)}), bf16[16,96,3,512]{3,1,0,2:T(8,128)(2,1)}) %all-gather.10.cloned.1.call-update) | async-done | bytes 4718608 | tf_op jit(solution)/shard_map/all_gather | solution.py:21
  104.5 0.3 broadcast_select_fusion
  104.8 6.7 copy.22
  111.6 12.3 %select_n.27 = bf16[4608,512]{1,0:T(8,128)(2,1)} reshape(bf16[4,4,96,3,512]{4,3,2,1,0:T(4,128)(2,1)} %copy.22) | data formatting | bytes 9437184 | tf_op jit(solution)/shard_map/jit(_where)/select_n | solution.py:40
  123.9 0.0 copy-start.1
  123.9 0.0 reduce-scatter.5.cloned.1.call-update
  123.9 0.0 all-gather.6.cloned.1.call-start
  124.0 109.4 %reduce-scatter.5.cloned.1.call-done = bf16[288,512]{1,0:T(8,128)(2,1)} async-done(((bf16[4608,512]{1,0:T(8,128)(2,1)}), bf16[288,512]{1,0:T(8,128)(2,1)}) %reduce-scatter.5.cloned.1.call-update) | async-done | bytes 294928 | tf_op jit(solution)/shard_map/reduce_scatter | solution.py:44
  233.4 0.0 all-gather.6.cloned.1.call-update
  233.4 0.0 reduce-scatter.7.cloned.1.call-start
  233.4 0.0 copy-done.1
  233.5 0.1 broadcast_bitcast_fusion
  233.6 0.1 copy.32
  233.8 79.2 %all-gather.6.cloned.1.call-done = bf16[4608,512]{1,0:T(8,128)(2,1)} async-done(((bf16[288,512]{1,0:T(8,128)(2,1)}), bf16[4608,512]{1,0:T(8,128)(2,1)}) %all-gather.6.cloned.1.call-update) | async-done | bytes 4718608 | tf_op jit(solution)/shard_map/all_gather | solution.py:45
  313.0 8.3 reshape.21
  321.3 6.6 copy.23
  327.9 2.6 bitcast_multiply_fusion
  330.6 11.9 %convolution_bitcast_fusion = f32[1536,1536]{0,1:T(8,128)} fusion(bf16[1536,1536]{0,1:T(8,128)(2,1)S(1)} %bitcast_multiply_fusion, bf16[1536,1536]{1,0:T(8,128)(2,1)} %param.4), kind=kOutput, calls=%fused_computation | convolution fusion | flops 7247757312 | bytes 18874368 | tf_op jit(solution)/shard_map/dot_general | solution.py:49
  342.5 9.6 %copy.28 = f32[1536,1536]{1,0:T(8,128)} copy(f32[1536,1536]{0,1:T(8,128)} %convolution_bitcast_fusion) | data formatting | bytes 18874368
  352.2 0.0 copy-start
  352.2 0.0 reduce-scatter.7.cloned.1.call-update
  352.2 0.0 all-reduce.3.cloned.1.call-start
  352.3 0.1 dynamic-slice_bitcast_fusion.1
  352.4 109.1 %reduce-scatter.7.cloned.1.call-done = f32[96,1536]{1,0:T(8,128)} async-done(((f32[1536,1536]{1,0:T(8,128)}), f32[96,1536]{1,0:T(8,128)}) %reduce-scatter.7.cloned.1.call-update) | async-done | bytes 589840
  461.4 1.3 copy.29
  462.7 0.1 neg.6
  462.8 0.0 copy-done
  462.8 3.3 fusion
  466.1 0.0 all-reduce.3.cloned.1.call-update
  466.1 0.0 all-reduce.5.cloned.1.call-start
  466.1 171.0 %all-reduce.3.cloned.1.call-done = f32[3,512,512]{2,1,0:T(8,128)} async-done(((f32[3,512,512]{2,1,0:T(8,128)}), f32[3,512,512]{2,1,0:T(8,128)}) %all-reduce.3.cloned.1.call-update) | async-done | bytes 3145744 | tf_op jit(solution)/shard_map/psum | solution.py:80
  637.2 0.0 all-reduce.5.cloned.1.call-update
  637.2 1.1 copy.25
  638.3 208.3 %all-reduce.5.cloned.1.call-done = f32[3,512,512]{2,1,0:T(8,128)} async-done(((f32[3,512,512]{2,1,0:T(8,128)}), f32[3,512,512]{2,1,0:T(8,128)}) %all-reduce.5.cloned.1.call-update) | async-done | bytes 3145744 | tf_op jit(solution)/shard_map/psum | solution.py:80
  846.5 5.3 sub.5
  (2 shorter events, 0.0 us)
Async XLA Ops:
  7.2 41.2 %all-gather.8.cloned.1.call-start = ((), (), s32[]{:S(2)}) async-start(), calls=%async_computation.6 | async-start | bytes 1474560 | tf_op jit(solution)/shard_map/all_gather | solution.py:21
  7.9 96.6 %all-gather.10.cloned.1.call-start = ((), (), s32[]{:S(2)}) async-start(), calls=%async_computation.7 | async-start | bytes 5898240 | tf_op jit(solution)/shard_map/all_gather | solution.py:21
  48.4 185.0 %reduce-scatter.5.cloned.1.call-start = ((), (), s32[]{:S(2)}) async-start(), calls=%async_computation.2 | async-start | bytes 5013504 | tf_op jit(solution)/shard_map/reduce_scatter | solution.py:44
  123.9 109.6 %copy-start.1 = (s32[3,192]{1,0:T(4,128)S(1)}, s32[3,192]{1,0:T(4,128)}, u32[]{:S(2)}) copy-start(s32[3,192]{1,0:T(4,128)} %param.7) | copy-start | bytes 6916
  123.9 189.1 %all-gather.6.cloned.1.call-start = ((), (), s32[]{:S(2)}) async-start(), calls=%async_computation.3 | async-start | bytes 5013504 | tf_op jit(solution)/shard_map/all_gather | solution.py:45
  233.4 228.0 %reduce-scatter.7.cloned.1.call-start = ((), (), s32[]{:S(2)}) async-start(), calls=%async_computation.8 | async-start | bytes 10027008
  352.2 110.6 %copy-start = (bf16[96,3,512]{2,0,1:T(8,128)(2,1)S(1)}, bf16[96,3,512]{2,0,1:T(8,128)(2,1)}, u32[]{:S(2)}) copy-start(bf16[96,3,512]{2,0,1:T(8,128)(2,1)} %param.5) | copy-start | bytes 884740
  352.2 284.9 %all-reduce.3.cloned.1.call-start = ((), (), s32[]{:S(2)}) async-start(), calls=%async_computation.4 | async-start | bytes 6291456 | tf_op jit(solution)/shard_map/psum | solution.py:80
  466.1 380.4 %all-reduce.5.cloned.1.call-start = ((), (), s32[]{:S(2)}) async-start(), calls=%async_computation.5 | async-start | bytes 6291456 | tf_op jit(solution)/shard_map/psum | solution.py:80
Sparse Core Ops, SparseCore 0:
  9.8 38.5 all-gather.7
  50.2 54.3 all-gather.9
  124.0 109.2 reduce-scatter.4
  236.3 76.6 all-gather.5
  352.3 109.0 reduce-scatter.6
  466.2 170.8 all-reduce.2
  640.0 206.4 all-reduce.4

commit v2 on v0

--- a/solution.py
+++ b/solution.py
@@ -42,7 +42,9 @@
     )
     padded = filled_up(lines, lax.axis_size(axis))
     own = lax.psum_scatter(padded, axis, scatter_dimension=0, tiled=True)
-    return lax.all_gather(own, axis, axis=0, tiled=True)[: len(lines)].reshape(shard.shape)
+    return jnp.concatenate(
+        lax.all_to_all(jnp.stack([own] * lax.axis_size(axis)), axis, 0, 0), axis=0
+    )[: len(lines)].reshape(shard.shape)
 
 
 def make_term(ancestor_inverse, right_side):

time: 743 us -> 777 us (1.046)
  waiting for transfers between devices: 658 us -> 681 us
    all_gather x1 -> x0, waiting for transfers between devices: 79.2 us -> none  [from_root(): lax.all_gather(own, axis, axis=0, tiled=True)[:len(lines)]]
    all_to_all x0 -> x1, waiting for transfers between devices: none -> 62.1 us  [from_root(): lax.all_to_all(jnp.stack([own] * lax.axis_size(axis)), axis, 0, 0)]
    unnamed x7 -> x6, waiting for transfers between devices: 110 us -> 150 us
    reshape x2 -> x0, local copies, waits for them, and re-layouts: 14.9 us -> none  [from_root(): lax.all_gather(own, axis, axis=0, tiled=True)[:len(lines)]]
    another operation x0 -> x2, local copies, waits for them, and re-layouts: none -> 11.9 us  [the longest x1 8.3 us: from_root(): return jnp.concatenate(lax.all_to_all(jnp.stack([own] * lax.axis_size(axi...]
    mul x0 -> x2, local copies, waits for them, and re-layouts: none -> 9.09 us  [body(): masked_col = partner * col_mask[:, :, None]]
  transfers between devices with their start and end apart: 6 -> 6, of which waited for: 6 -> 6; matrix products, arithmetic and copies ran while one was open for 0% -> 1% of each run, Pallas kernels for 0% -> 0%
where the time goes in v2:
time: 777 us; the launch traced here: 776 us
  waiting for transfers between devices  681 us (88%)
  local copies, waits for them, and re-layouts  52.4 us (7%)
  matrix products  18.3 us (2%)
  between operations  13.9 us (2%)
    psum x1, waiting for transfers between devices, body(): schur_total = lax.psum(schur_part, ROW_COL)  263 us
    unnamed x6, waiting for transfers between devices  150 us
    reduce_scatter x1, waiting for transfers between devices, from_root(): own = lax.psum_scatter(padded, axis, scatter_dimension=0, tiled=True)  109 us
    all_gather x2, waiting for transfers between devices, stacked_from(): tiles = lax.all_gather(tiles, axes[k])  96.5 us
    all_to_all x1, waiting for transfers between devices, from_root(): lax.all_to_all(jnp.stack([own] * lax.axis_size(axis)), axis, 0, 0)  62.1 us
    select_n x2, local copies, waits for them, and re-layouts, from_root(): jnp.where(lax.axis_index(axis) == root, shard, jnp.zeros_like(shard))  19.1 us
  transfers between devices with their start and end apart: 6, of which 6 were waited for; matrix products, arithmetic and copies ran while one was open for 1% of the time, Pallas kernels for 0%

profile of v2, /device:TPU:2, one launch (start us, length us, event | category | flops | bytes accessed | tf_op | source)
XLA Modules:
  0.0 776.5 jit_solution(1082534950995831918)
XLA Ops:
  7.2 0.0 all-gather.5.cloned.1.call-start
  7.2 0.7 all-gather.5.cloned.1.call-update
  7.9 0.0 all-gather.7.cloned.1.call-start
  7.9 40.4 %all-gather.5.cloned.1.call-done = bf16[384,3,512]{2,0,1:T(8,128)(2,1)} async-done(((bf16[96,3,512]{2,0,1:T(8,128)(2,1)}), bf16[384,3,512]{2,0,1:T(8,128)(2,1)}) %all-gather.5.cloned.1.call-update) | async-done | bytes 1179664 | tf_op jit(solution)/shard_map/all_gather | solution.py:21
  48.4 0.0 all-gather.7.cloned.1.call-update
  48.4 0.0 reduce-scatter.5.cloned.1.call-start
  48.4 56.1 %all-gather.7.cloned.1.call-done = bf16[16,96,3,512]{3,1,0,2:T(8,128)(2,1)} async-done(((bf16[4,96,3,512]{3,1,0,2:T(8,128)(2,1)}), bf16[16,96,3,512]{3,1,0,2:T(8,128)(2,1)}) %all-gather.7.cloned.1.call-update) | async-done | bytes 4718608 | tf_op jit(solution)/shard_map/all_gather | solution.py:21
  104.5 0.3 broadcast_select_fusion
  104.8 6.7 copy.21
  111.6 12.3 %select_n.27 = bf16[4608,512]{1,0:T(8,128)(2,1)} reshape(bf16[4,4,96,3,512]{4,3,2,1,0:T(4,128)(2,1)} %copy.21) | data formatting | bytes 9437184 | tf_op jit(solution)/shard_map/jit(_where)/select_n | solution.py:40
  123.9 0.0 reduce-scatter.5.cloned.1.call-update
  123.9 109.5 %reduce-scatter.5.cloned.1.call-done = bf16[288,512]{1,0:T(8,128)(2,1)} async-done(((bf16[4608,512]{1,0:T(8,128)(2,1)}), bf16[288,512]{1,0:T(8,128)(2,1)}) %reduce-scatter.5.cloned.1.call-update) | async-done | bytes 294928 | tf_op jit(solution)/shard_map/reduce_scatter | solution.py:44
  233.4 3.6 stack.2
  237.0 0.0 copy-start.1
  237.0 5.3 all-to-all-start
  242.3 0.0 reduce-scatter.7.cloned.1.call-start
  242.3 0.0 copy-done.1
  242.3 0.1 broadcast_bitcast_fusion
  242.5 0.1 copy.31
  242.6 2.4 mul.33
  245.1 6.6 copy.22
  251.7 62.1 %all-to-all-done = bf16[16,288,512]{2,1,0:T(8,128)(2,1)} async-done(((bf16[16,288,512]{2,1,0:T(8,128)(2,1)}), bf16[16,288,512]{2,1,0:T(8,128)(2,1)}, u32[]{:S(2)}, u32[]{:S(2)}) %all-to-all-start) | async-done | bytes 4718624 | tf_op jit(solution)/shard_map/all_to_all | solution.py:46
  313.8 8.3 %reshape_reshape.4 = bf16[1536,1536]{1,0:T(8,128)(2,1)} reshape(bf16[16,288,512]{2,1,0:T(8,128)(2,1)} %all-to-all-done) | data formatting | bytes 9437184 | tf_op jit(solution)/shard_map/reshape;reshape | solution.py:47
  322.1 15.1 %convolution_bitcast_fusion = f32[1536,1536]{0,1:T(8,128)} fusion(bf16[1536,1536]{1,0:T(8,128)(2,1)} %param.4, bf16[1536,1536]{1,0:T(8,128)(2,1)} %reshape_reshape.4, bf16[1536,1536]{1,0:T(8,128)(2,1)} %copy.22), kind=kOutput, calls=%fused_computation | convolution fusion | flops 7250116608 | bytes 23592960 | tf_op jit(solution)/shard_map/dot_general | solution.py:51
  337.2 9.6 %copy.27 = f32[1536,1536]{1,0:T(8,128)} copy(f32[1536,1536]{0,1:T(8,128)} %convolution_bitcast_fusion) | data formatting | bytes 18874368
  346.8 0.0 copy-start
  346.8 0.0 reduce-scatter.7.cloned.1.call-update
  346.8 0.2 all-reduce.2.cloned.1.call-start
  347.0 0.1 dynamic-slice_bitcast_fusion.1
  347.1 149.2 %reduce-scatter.7.cloned.1.call-done = f32[96,1536]{1,0:T(8,128)} async-done(((f32[1536,1536]{1,0:T(8,128)}), f32[96,1536]{1,0:T(8,128)}) %reduce-scatter.7.cloned.1.call-update) | async-done | bytes 589840
  496.3 1.3 copy.28
  497.6 0.1 neg.6
  497.7 0.0 copy-done
  497.7 3.2 fusion.1
  500.9 0.0 all-reduce.2.cloned.1.call-update
  501.0 1.1 copy.24
  502.0 262.6 %all-reduce.2.cloned.1.call-done = f32[3,512,512]{2,1,0:T(8,128)} async-done(((f32[3,512,512]{2,1,0:T(8,128)}), f32[3,512,512]{2,1,0:T(8,128)}) %all-reduce.2.cloned.1.call-update) | async-done | bytes 3145744 | tf_op jit(solution)/shard_map/psum | solution.py:82
  764.7 5.3 sub.5
  (2 shorter events, 0.0 us)
Async XLA Ops:
  7.2 41.2 %all-gather.5.cloned.1.call-start = ((), (), s32[]{:S(2)}) async-start(), calls=%async_computation.5 | async-start | bytes 1474560 | tf_op jit(solution)/shard_map/all_gather | solution.py:21
  7.9 96.6 %all-gather.7.cloned.1.call-start = ((), (), s32[]{:S(2)}) async-start(), calls=%async_computation.6 | async-start | bytes 5898240 | tf_op jit(solution)/shard_map/all_gather | solution.py:21
  48.4 185.0 %reduce-scatter.5.cloned.1.call-start = ((), (), s32[]{:S(2)}) async-start(), calls=%async_computation.3 | async-start | bytes 5013504 | tf_op jit(solution)/shard_map/reduce_scatter | solution.py:44
  237.0 5.3 copy-start.1
  237.0 76.8 %all-to-all-start = ((bf16[16,288,512]{2,1,0:T(8,128)(2,1)}), bf16[16,288,512]{2,1,0:T(8,128)(2,1)}, u32[]{:S(2)}, u32[]{:S(2)}) async-start(bf16[16,288,512]{2,1,0:T(8,128)(2,1)} %stack.2), calls=%async_computation.1 | async-start | bytes 9437184 | tf_op jit(solution)/shard_map/all_to_all | solution.py:46
  242.3 254.0 %reduce-scatter.7.cloned.1.call-start = ((), (), s32[]{:S(2)}) async-start(), calls=%async_computation.7 | async-start | bytes 10027008
  346.8 150.9 %copy-start = (bf16[96,3,512]{2,0,1:T(8,128)(2,1)S(1)}, bf16[96,3,512]{2,0,1:T(8,128)(2,1)}, u32[]{:S(2)}) copy-start(bf16[96,3,512]{2,0,1:T(8,128)(2,1)} %param.5) | copy-start | bytes 884740
  346.8 417.9 %all-reduce.2.cloned.1.call-start = ((), (), s32[]{:S(2)}) async-start(), calls=%async_computation.4 | async-start | bytes 6291456 | tf_op jit(solution)/shard_map/psum | solution.py:82
Sparse Core Ops, SparseCore 0:
  9.8 38.5 all-gather.4
  50.2 54.3 all-gather.6
  124.0 109.2 reduce-scatter.4
  346.9 149.3 reduce-scatter.6
  503.0 261.6 all-reduce.1
